TPU v7x, 32 devices: a whole 2x2x4 slice. The times are simulated.
32 devices in a mesh: section: 4 (over z), ep: 8 (over y, x, core).
Axes of the slice: x: 2, y: 2, z: 4, core: 2. Of those that a mesh axis runs over, the one named last changes fastest.
Arguments:
- flight_a: bfloat16 [4, 1024, 3584], P('section', 'ep'), may hold values from -6 to 6
- flight_b: bfloat16 [4, 1024, 3584], P('section', 'ep'), may hold values from -6 to 6
- routes_a: int32 [4, 1, 1024, 1], P('section', None, 'ep'), may hold values from 0 to 1; in each aligned block of 128 rows (0 to 127, 128 to 255, ..., all dimensions but the last counted through in order) at most 72 rows name the same one
- routes_b: int32 [4, 1, 1024, 1], P('section', None, 'ep'), may hold values from 0 to 1; in each aligned block of 128 rows (0 to 127, 128 to 255, ..., all dimensions but the last counted through in order) at most 72 rows name the same one
- scores_a: float32 [4, 1, 1024, 1], P('section', None, 'ep'), may hold values from 0.5 to 1.5
- scores_b: float32 [4, 1, 1024, 1], P('section', None, 'ep'), may hold values from 0.5 to 1.5
- norm_gain: float32 [4, 3584], P('section'), may hold values from 0.1 to 1.9
- w_gate: bfloat16 [4, 3584, 2048], P('section', None, 'ep'), may hold values from -0.09375 to 0.09375
- w_up: bfloat16 [4, 3584, 2048], P('section', None, 'ep'), may hold values from -0.09375 to 0.09375
- w_down: bfloat16 [4, 2048, 3584], P('section', 'ep'), may hold values from -0.1875 to 0.1875
Outputs:
- out_a: bfloat16 [4, 1024, 3584], P('section', 'ep')
- out_b: bfloat16 [4, 1024, 3584], P('section', 'ep')
Inputs may be any that keep to these rules, and one draw needn't show every extreme that they name: `routes_a`: in each block of 128 rows that one device holds for one layer and step, no expert is named more than 72 times, a bound that some block reaches; a row never names one expert twice. `routes_b`: as for routes_a.
All inputs are finite; a program needn't handle non-finite values.
Results may differ from a plain program's by a relative error of at most 0.0054.
Values may be sent and summed in bfloat16 or wider, within the bound.
A program may use at most 128 MiB of HBM per device.

v0:
```python
import jax
import jax.numpy as jnp
from jax import lax
from jax.sharding import PartitionSpec as P

ES = 4
TOPK = 1
EPSILON = 1e-06


def from_behind(value, axis, steps):
    count = lax.axis_size(axis)
    pairs = [(source, (source + steps) % count) for source in range(count)]
    return lax.ppermute(value, axis, pairs)


def rms_norm(current, gain):
    as_float = current.astype(jnp.float32)
    inverse_rms = lax.rsqrt(jnp.mean(as_float * as_float, axis=-1, keepdims=True) + EPSILON)
    return (as_float * inverse_rms * gain).astype(jnp.bfloat16)


def routing(expert_ids, route_weights, expert_count, capacity):
    token_count, top_count = expert_ids.shape
    flat_ids = expert_ids.reshape(token_count * top_count)
    onehot = (flat_ids[:, None] == jnp.arange(expert_count, dtype=jnp.int32)[None, :]).astype(
        jnp.int32
    )
    before = jnp.cumsum(onehot, axis=0) - onehot
    slot_index = jnp.sum(before * onehot, axis=1)
    column = flat_ids * capacity + slot_index
    placed = column[:, None] == jnp.arange(expert_count * capacity, dtype=jnp.int32)[None, :]
    placed = placed.reshape(token_count, top_count, expert_count * capacity)
    picker = jnp.any(placed, axis=1).astype(jnp.bfloat16)
    mixing = jnp.sum(jnp.where(placed, route_weights[:, :, None], 0.0), axis=1)
    return (picker, mixing)


def prepare(current, expert_ids, route_weights, gain, expert_count, capacity):
    normed = rms_norm(current, gain)
    picker, mixing = routing(expert_ids, route_weights, expert_count, capacity)
    feature_width = normed.shape[1]
    slotted = jnp.einsum("ts,td->sd", picker, normed, preferred_element_type=jnp.float32).astype(
        jnp.bfloat16
    )
    slotted = slotted.reshape(expert_count, 1, capacity, feature_width)
    outgoing = jnp.broadcast_to(slotted, (expert_count, ES, capacity, feature_width))
    return (outgoing.reshape(expert_count * ES, capacity, feature_width), mixing)


def expert_pass(outgoing, gate_cols, up_cols, down_part):
    received = lax.all_to_all(outgoing, "ep", split_axis=0, concat_axis=0, tiled=True)
    source_count, slot_count, feature_width = received.shape
    row_block = received.reshape(source_count * slot_count, feature_width)
    gate_act = jnp.dot(row_block, gate_cols, preferred_element_type=jnp.float32)
    up_act = jnp.dot(row_block, up_cols, preferred_element_type=jnp.float32)
    hidden = (jax.nn.silu(gate_act) * up_act).astype(jnp.bfloat16)
    partial_value = jnp.dot(hidden, down_part, preferred_element_type=jnp.float32).astype(
        jnp.bfloat16
    )
    partial_value = partial_value.reshape(source_count, slot_count, feature_width)
    return lax.all_to_all(partial_value, "ep", split_axis=0, concat_axis=0, tiled=True)


def finish(current, returned, mixing, expert_count):
    feature_width = current.shape[1]
    slot_count = returned.shape[1]
    by_slice = returned.astype(jnp.float32).reshape(expert_count, ES, slot_count, feature_width)
    summed = jnp.sum(by_slice, axis=1).reshape(expert_count * slot_count, feature_width)
    moe_out = jnp.dot(
        mixing, summed, precision=lax.Precision.HIGHEST, preferred_element_type=jnp.float32
    )
    return (current.astype(jnp.float32) + moe_out).astype(jnp.bfloat16)


def on_device(
    flight_a, flight_b, routes_a, routes_b, scores_a, scores_b, norm_gain, w_gate, w_up, w_down
):
    ep_count = lax.axis_size("ep")
    expert_count = ep_count // ES
    tok_dev = flight_a.shape[1]
    capacity = min(tok_dev, 9 * tok_dev * TOPK * ES // (8 * ep_count))
    section_index = lax.axis_index("section")
    last_section = lax.axis_size("section") - 1
    gain = norm_gain[0]
    gate_cols = w_gate[0]
    up_cols = w_up[0]
    down_part = w_down[0]
    current_a = flight_a[0]
    current_b = flight_b[0]
    outgoing_a, mixing_a = prepare(
        current_a, routes_a[0, 0], scores_a[0, 0], gain, expert_count, capacity
    )
    outgoing_b, mixing_b = prepare(
        current_b, routes_b[0, 0], scores_b[0, 0], gain, expert_count, capacity
    )
    returned_a = expert_pass(outgoing_a, gate_cols, up_cols, down_part)
    returned_b = expert_pass(outgoing_b, gate_cols, up_cols, down_part)
    updated_a = finish(current_a, returned_a, mixing_a, expert_count)
    updated_b = finish(current_b, returned_b, mixing_b, expert_count)
    current_a = jnp.where(0 <= section_index, updated_a, current_a)
    current_b = jnp.where(section_index + 0 <= last_section, updated_b, current_b)
    current_a = from_behind(current_a, "section", 1)
    current_b = from_behind(current_b, "section", -1)
    return (current_a[None], current_b[None])


def solution(mesh):
    placed = (
        P("section", "ep", None),
        P("section", "ep", None),
        P("section", None, "ep", None),
        P("section", None, "ep", None),
        P("section", None, "ep", None),
        P("section", None, "ep", None),
        P("section", None),
        P("section", None, "ep"),
        P("section", None, "ep"),
        P("section", "ep", None),
    )
    return jax.shard_map(
        on_device,
        mesh=mesh,
        in_specs=placed,
        out_specs=(P("section", "ep", None), P("section", "ep", None)),
        check_vma=False,
    )
```

profile of v0, /device:TPU:2, one launch (start us, length us, event | category | flops | bytes accessed | tf_op | source)
XLA Modules:
  0.0 256.0 jit_solution(12852984667697311953)
XLA Ops:
  0.6 0.9 fusion.60
  1.5 0.2 reduce_window_sum.18
  1.7 0.8 select_reduce_fusion
  2.5 0.7 multiply_add_fusion
  3.2 1.4 fusion.5
  4.6 0.8 reduce
  5.4 1.7 convolution_convert_fusion.2
  7.1 2.2 broadcast_in_dim.59
  9.3 4.6 %all-to-all-start.2 = ((bf16[8,72,3584]{2,1,0:T(8,128)(2,1)}), bf16[8,72,3584]{2,1,0:T(8,128)(2,1)}, u32[]{:S(2)}, u32[]{:S(2)}) async-start(bf16[8,72,3584]{2,1,0:T(8,128)(2,1)} %bitcast.81), calls=%async_computation.2 | async-start | bytes 8257536 | tf_op jit(solution)/shard_map/all_to_all | solution.py:52
  14.4 0.3 fusion.4
  14.7 1.6 convolution_convert_fusion.3
  16.3 44.4 %all-to-all-done.2 = bf16[8,72,3584]{2,1,0:T(8,128)(2,1)} async-done(((bf16[8,72,3584]{2,1,0:T(8,128)(2,1)}), bf16[8,72,3584]{2,1,0:T(8,128)(2,1)}, u32[]{:S(2)}, u32[]{:S(2)}) %all-to-all-start.2) | async-done | bytes 4128800 | tf_op jit(solution)/shard_map/all_to_all | solution.py:52
  60.7 3.4 %broadcast_in_dim.54 = bf16[2,4,72,3584]{3,2,1,0:T(8,128)(2,1)} broadcast(bf16[2,72,3584]{2,1,0:T(8,128)(2,1)} %bitcast.85), dimensions={0,2,3} | broadcast | bytes 5160960 | tf_op jit(solution)/shard_map/broadcast_in_dim | solution.py:47
  64.1 5.9 %all-to-all-start = ((bf16[8,72,3584]{2,1,0:T(8,128)(2,1)}), bf16[8,72,3584]{2,1,0:T(8,128)(2,1)}, u32[]{:S(2)}, u32[]{:S(2)}) async-start(bf16[8,72,3584]{2,1,0:T(8,128)(2,1)} %bitcast.82), calls=%async_computation | async-start | bytes 8257536 | tf_op jit(solution)/shard_map/all_to_all | solution.py:52
  70.1 4.0 %fusion.12 = f32[576,256]{1,0:T(8,128)S(1)} fusion(bf16[576,3584]{1,0:T(8,128)(2,1)} %bitcast.24, bf16[1,3584,256]{2,1,0:T(8,128)(2,1)} %param.17), kind=kOutput, calls=%fused_computation.22 | convolution fusion | flops 1056964608 | bytes 6553600 | tf_op jit(solution)/shard_map/dot_general | solution.py:55
  74.1 9.1 %convolution_convert_fusion = bf16[576,3584]{1,0:T(8,128)(2,1)} fusion(bf16[1,256,3584]{2,1,0:T(8,128)(2,1)S(1)} %copy-done, bf16[576,3584]{1,0:T(8,128)(2,1)} %bitcast.24, bf16[1,3584,256]{2,1,0:T(8,128)(2,1)} %param.18, f32[576,256]{1,0:T(8,128)S(1)} %fusion.12), kind=kOutput, calls=%fused_computation.2 | convolution fusion | flops 2116878336 | bytes 12517376 | tf_op jit(solution)/shard_map/dot_general | solution.py:58
  83.2 33.9 %all-to-all-done = bf16[8,72,3584]{2,1,0:T(8,128)(2,1)} async-done(((bf16[8,72,3584]{2,1,0:T(8,128)(2,1)}), bf16[8,72,3584]{2,1,0:T(8,128)(2,1)}, u32[]{:S(2)}, u32[]{:S(2)}) %all-to-all-start) | async-done | bytes 4128800 | tf_op jit(solution)/shard_map/all_to_all | solution.py:52
  117.1 6.0 %all-to-all-start.3 = ((bf16[8,72,3584]{2,1,0:T(8,128)(2,1)}), bf16[8,72,3584]{2,1,0:T(8,128)(2,1)}, u32[]{:S(2)}, u32[]{:S(2)}) async-start(bf16[8,72,3584]{2,1,0:T(8,128)(2,1)} %bitcast.88), calls=%async_computation.3 | async-start | bytes 8257536 | tf_op jit(solution)/shard_map/all_to_all | solution.py:62
  123.0 4.0 %fusion.14 = f32[576,256]{1,0:T(8,128)S(1)} fusion(bf16[576,3584]{1,0:T(8,128)(2,1)} %bitcast.8, bf16[1,3584,256]{2,1,0:T(8,128)(2,1)} %param.17), kind=kOutput, calls=%fused_computation.24 | convolution fusion | flops 1056964608 | bytes 6553600 | tf_op jit(solution)/shard_map/dot_general | solution.py:55
  127.0 9.1 %convolution_convert_fusion.1 = bf16[576,3584]{1,0:T(8,128)(2,1)} fusion(bf16[1,256,3584]{2,1,0:T(8,128)(2,1)S(1)} %copy-done, bf16[576,3584]{1,0:T(8,128)(2,1)} %bitcast.8, bf16[1,3584,256]{2,1,0:T(8,128)(2,1)} %param.18, f32[576,256]{1,0:T(8,128)S(1)} %fusion.14), kind=kOutput, calls=%fused_computation.3 | convolution fusion | flops 2116878336 | bytes 12517376 | tf_op jit(solution)/shard_map/dot_general | solution.py:58
  136.1 33.9 %all-to-all-done.3 = bf16[8,72,3584]{2,1,0:T(8,128)(2,1)} async-done(((bf16[8,72,3584]{2,1,0:T(8,128)(2,1)}), bf16[8,72,3584]{2,1,0:T(8,128)(2,1)}, u32[]{:S(2)}, u32[]{:S(2)}) %all-to-all-start.3) | async-done | bytes 4128800 | tf_op jit(solution)/shard_map/all_to_all | solution.py:62
  170.0 5.9 %all-to-all-start.1 = ((bf16[8,72,3584]{2,1,0:T(8,128)(2,1)}), bf16[8,72,3584]{2,1,0:T(8,128)(2,1)}, u32[]{:S(2)}, u32[]{:S(2)}) async-start(bf16[8,72,3584]{2,1,0:T(8,128)(2,1)} %bitcast.87), calls=%async_computation.1 | async-start | bytes 8257536 | tf_op jit(solution)/shard_map/all_to_all | solution.py:62
  176.0 3.1 %convert_reduce_fusion = f32[2,72,3584]{2,1,0:T(8,128)S(1)} fusion(bf16[8,72,3584]{2,1,0:T(8,128)(2,1)} %all-to-all-done.3), kind=kLoop, calls=%fused_computation | loop fusion | flops 3612672 | bytes 6193152 | tf_op jit(solution)/shard_map/reduce_sum | solution.py:69
  179.1 2.8 %fusion.2 = bf16[128,3584]{1,0:T(8,128)(2,1)} fusion(f32[144,3584]{1,0:T(8,128)S(1)} %bitcast.83, bf16[1,128,3584]{2,1,0:T(8,128)(2,1)S(1)} %copy-done.1, pred[]{:T(512)S(6)} %le.3, f32[128]{0:T(128)S(1)} %bitcast.94, s32[128]{0:T(128)S(1)} %multiply_add_fusion), kind=kOutput, calls=%fused_computation.10 | convolution fusion | flops 794595328 | bytes 3900417 | tf_op jit(solution)/shard_map/dot_general | solution.py:70
  182.0 4.3 %collective-permute-start.1 = (bf16[128,3584]{1,0:T(8,128)(2,1)}, bf16[128,3584]{1,0:T(8,128)(2,1)}, u32[]{:S(2)}, u32[]{:S(2)}) collective-permute-start(bf16[128,3584]{1,0:T(8,128)(2,1)} %fusion.2), channel_id=1, source_target_pairs={{0,24},{8,0},{16,8},{24,16},{1,25},{9,1},{17,9},{25,17},{2,26},{10... | collective-permute-start | bytes 2752520 | tf_op jit(solution)/shard_map/ppermute | solution.py:14
  186.3 36.7 %all-to-all-done.1 = bf16[8,72,3584]{2,1,0:T(8,128)(2,1)} async-done(((bf16[8,72,3584]{2,1,0:T(8,128)(2,1)}), bf16[8,72,3584]{2,1,0:T(8,128)(2,1)}, u32[]{:S(2)}, u32[]{:S(2)}) %all-to-all-start.1) | async-done | bytes 4128800 | tf_op jit(solution)/shard_map/all_to_all | solution.py:62
  223.0 3.1 %convert_reduce_fusion.1 = f32[2,72,3584]{2,1,0:T(8,128)S(1)} fusion(bf16[8,72,3584]{2,1,0:T(8,128)(2,1)} %all-to-all-done.1), kind=kLoop, calls=%fused_computation.1 | loop fusion | flops 3612672 | bytes 6193152 | tf_op jit(solution)/shard_map/reduce_sum | solution.py:69
  226.0 1.9 fusion.3
  228.0 2.4 collective-permute-start
  230.3 22.6 %collective-permute-done = bf16[128,3584]{1,0:T(8,128)(2,1)S(1)} collective-permute-done((bf16[128,3584]{1,0:T(8,128)(2,1)S(1)}, bf16[128,3584]{1,0:T(8,128)(2,1)S(1)}, u32[]{:S(2)}, u32[]{:S(2)}) %collective-permute-start) | collective-permute-done | bytes 917536 | tf_op jit(solution)/shard_map/ppermute | solution.py:14
  252.9 0.9 copy.14
  253.9 2.2 copy.15
  (19 shorter events, 0.5 us)
Async XLA Ops:
  0.6 73.4 %copy-start = (bf16[1,256,3584]{2,1,0:T(8,128)(2,1)S(1)}, bf16[1,256,3584]{2,1,0:T(8,128)(2,1)}, u32[]{:S(2)}) copy-start(bf16[1,256,3584]{2,1,0:T(8,128)(2,1)} %param.19) | copy-start | bytes 5505028
  9.3 4.6 %copy-start.3 = (s32[1,1,128,1]{2,3,1,0:T(1,128)S(1)}, s32[1,1,128,1]{2,3,1,0:T(1,128)}, u32[]{:S(2)}) copy-start(s32[1,1,128,1]{2,3,1,0:T(1,128)} %param.12) | copy-start | bytes 1540
  9.3 5.1 %copy-start.2 = (bf16[1,128,3584]{2,1,0:T(8,128)(2,1)S(1)}, bf16[1,128,3584]{2,1,0:T(8,128)(2,1)}, u32[]{:S(2)}) copy-start(bf16[1,128,3584]{2,1,0:T(8,128)(2,1)} %param.10) | copy-start | bytes 2752516
  9.3 51.4 %all-to-all-start.2 = ((bf16[8,72,3584]{2,1,0:T(8,128)(2,1)}), bf16[8,72,3584]{2,1,0:T(8,128)(2,1)}, u32[]{:S(2)}, u32[]{:S(2)}) async-start(bf16[8,72,3584]{2,1,0:T(8,128)(2,1)} %bitcast.81), calls=%async_computation.2 | async-start | bytes 8257536 | tf_op jit(solution)/shard_map/all_to_all | solution.py:52
  64.1 52.9 %all-to-all-start = ((bf16[8,72,3584]{2,1,0:T(8,128)(2,1)}), bf16[8,72,3584]{2,1,0:T(8,128)(2,1)}, u32[]{:S(2)}, u32[]{:S(2)}) async-start(bf16[8,72,3584]{2,1,0:T(8,128)(2,1)} %bitcast.82), calls=%async_computation | async-start | bytes 8257536 | tf_op jit(solution)/shard_map/all_to_all | solution.py:52
  117.1 53.0 %all-to-all-start.3 = ((bf16[8,72,3584]{2,1,0:T(8,128)(2,1)}), bf16[8,72,3584]{2,1,0:T(8,128)(2,1)}, u32[]{:S(2)}, u32[]{:S(2)}) async-start(bf16[8,72,3584]{2,1,0:T(8,128)(2,1)} %bitcast.88), calls=%async_computation.3 | async-start | bytes 8257536 | tf_op jit(solution)/shard_map/all_to_all | solution.py:62
  170.0 52.9 %all-to-all-start.1 = ((bf16[8,72,3584]{2,1,0:T(8,128)(2,1)}), bf16[8,72,3584]{2,1,0:T(8,128)(2,1)}, u32[]{:S(2)}, u32[]{:S(2)}) async-start(bf16[8,72,3584]{2,1,0:T(8,128)(2,1)} %bitcast.87), calls=%async_computation.1 | async-start | bytes 8257536 | tf_op jit(solution)/shard_map/all_to_all | solution.py:62
  176.0 3.1 %copy-start.1 = (bf16[1,128,3584]{2,1,0:T(8,128)(2,1)S(1)}, bf16[1,128,3584]{2,1,0:T(8,128)(2,1)}, u32[]{:S(2)}) copy-start(bf16[1,128,3584]{2,1,0:T(8,128)(2,1)} %param.11) | copy-start | bytes 2752516
  176.0 3.1 %copy-start.4 = (f32[1,1,128,1]{2,3,1,0:T(1,128)S(1)}, f32[1,1,128,1]{2,3,1,0:T(1,128)}, u32[]{:S(2)}) copy-start(f32[1,1,128,1]{2,3,1,0:T(1,128)} %param.15) | copy-start | bytes 1540
  182.0 44.1 %copy-start.5 = (f32[1,1,128,1]{2,3,1,0:T(1,128)S(1)}, f32[1,1,128,1]{2,3,1,0:T(1,128)}, u32[]{:S(2)}) copy-start(f32[1,1,128,1]{2,3,1,0:T(1,128)} %param.14) | copy-start | bytes 1540
  182.0 48.4 %collective-permute-start.1 = (bf16[128,3584]{1,0:T(8,128)(2,1)}, bf16[128,3584]{1,0:T(8,128)(2,1)}, u32[]{:S(2)}, u32[]{:S(2)}) collective-permute-start(bf16[128,3584]{1,0:T(8,128)(2,1)} %fusion.2), channel_id=1, source_target_pairs={{0,24},{8,0},{16,8},{24,16},{1,25},{9,1},{17,9},{25,17},{2,26},{10... | collective-permute-start | bytes 2752520 | tf_op jit(solution)/shard_map/ppermute | solution.py:14
  228.0 25.0 %collective-permute-start = (bf16[128,3584]{1,0:T(8,128)(2,1)S(1)}, bf16[128,3584]{1,0:T(8,128)(2,1)S(1)}, u32[]{:S(2)}, u32[]{:S(2)}) collective-permute-start(bf16[128,3584]{1,0:T(8,128)(2,1)S(1)} %fusion.3), channel_id=1, source_target_pairs={{0,8},{8,16},{16,24},{24,0},{1,9},{9,17},{17,25},{25,1},{2,10},{10... | collective-permute-start | bytes 2752520 | tf_op jit(solution)/shard_map/ppermute | solution.py:14
where the time goes:
time: 257 us; the launch traced here: 256 us
  waiting for transfers between devices  172 us (67%)
  matrix products  34.2 us (13%)
  starting transfers between devices  29.2 us (11%)
  other arithmetic  11.6 us (5%)
  local copies, waits for them, and re-layouts  8.78 us (3%)
    all_to_all x2, waiting for transfers between devices, expert_pass(): lax.all_to_all(outgoing, 'ep', split_axis=0, concat_axis=0, tiled=True)  78.3 us
    all_to_all x2, waiting for transfers between devices, expert_pass(): lax.all_to_all(partial_value, 'ep', split_axis=0, concat_axis=0, tiled=True)  70.6 us
    ppermute x2, waiting for transfers between devices, from_behind(): return lax.ppermute(value, axis, pairs)  22.6 us
    dot_general x2, matrix products, expert_pass(): jnp.dot(hidden, down_part, preferred_element_type=jnp.float32)  18.2 us
    all_to_all x2, starting transfers between devices, expert_pass(): lax.all_to_all(partial_value, 'ep', split_axis=0, concat_axis=0, tiled=True)  11.9 us
    all_to_all x2, starting transfers between devices, expert_pass(): lax.all_to_all(outgoing, 'ep', split_axis=0, concat_axis=0, tiled=True)  10.6 us
    dot_general x2, matrix products, expert_pass(): gate_act = jnp.dot(row_block, gate_cols, preferred_element_type=jnp.float32)  7.95 us
    ppermute x2, starting transfers between devices, from_behind(): return lax.ppermute(value, axis, pairs)  6.69 us
  transfers between devices with their start and end apart: 6, of which 5 were waited for; matrix products, arithmetic and copies ran while one was open for 15% of the time, Pallas kernels for 0%

commit v1 on v0

--- a/solution.py
+++ b/solution.py
@@ -6,6 +6,28 @@
 ES = 4
 TOPK = 1
 EPSILON = 1e-06
+
+
+def cut_along(x, dim, size):
+    before, after = (x.shape[:dim], x.shape[dim + 1 :])
+    return jnp.moveaxis(x.reshape(*before, size, -1, *after), dim, 0)
+
+
+def joined_along(parts, dim):
+    lengths = list(parts.shape[1:])
+    lengths[dim] *= parts.shape[0]
+    return jnp.moveaxis(parts, 0, dim).reshape(lengths)
+
+
+def exchange_in_pairs(array, axis, split_dim, concat_dim):
+    devices, here = (lax.axis_size(axis), lax.axis_index(axis))
+    tiles = cut_along(array, split_dim, devices)
+    gathered = [tiles[here]]
+    for turn in range(1, devices):
+        sent = tiles[here ^ turn]
+        gathered.append(lax.ppermute(sent, axis, [(i, i ^ turn) for i in range(devices)]))
+    tiles = jnp.stack(gathered)[here ^ jnp.arange(devices)]
+    return joined_along(tiles, concat_dim)
 
 
 def from_behind(value, axis, steps):
@@ -49,7 +71,7 @@
 
 
 def expert_pass(outgoing, gate_cols, up_cols, down_part):
-    received = lax.all_to_all(outgoing, "ep", split_axis=0, concat_axis=0, tiled=True)
+    received = exchange_in_pairs(outgoing, "ep", 0, 0)
     source_count, slot_count, feature_width = received.shape
     row_block = received.reshape(source_count * slot_count, feature_width)
     gate_act = jnp.dot(row_block, gate_cols, preferred_element_type=jnp.float32)

time: 257 us -> 263 us (1.023)
  local copies, waits for them, and re-layouts: 8.78 us -> 39 us
  waiting for transfers between devices: 172 us -> 148 us
    ppermute x0 -> x14, waiting for transfers between devices: none -> 87.8 us  [exchange_in_pairs(): lax.ppermute(sent, axis, [(i, i ^ turn) for i in range(devices)])]
    all_to_all x2 -> x0, waiting for transfers between devices: 78.3 us -> none  [expert_pass(): lax.all_to_all(outgoing, 'ep', split_axis=0, concat_axis=0, tiled=True)]
    all_to_all x2, waiting for transfers between devices: 70.6 us -> 37.4 us  [expert_pass(): lax.all_to_all(partial_value, 'ep', split_axis=0, concat_axis=0, tiled=True)]
    unnamed x14 -> x32, local copies, waits for them, and re-layouts: 3.11 us -> 23.5 us
    ppermute x0 -> x14, starting transfers between devices: none -> 11.4 us  [exchange_in_pairs(): lax.ppermute(sent, axis, [(i, i ^ turn) for i in range(devices)])]
    all_to_all x2 -> x0, starting transfers between devices: 10.6 us -> none  [expert_pass(): lax.all_to_all(outgoing, 'ep', split_axis=0, concat_axis=0, tiled=True)]
    gather x0 -> x2, local copies, waits for them, and re-layouts: none -> 9.79 us  [exchange_in_pairs(): tiles = jnp.stack(gathered)[here ^ jnp.arange(devices)]]
    broadcast_in_dim x2, local copies, waits for them, and re-layouts: 5.67 us -> 0.57 us  [prepare(): jnp.broadcast_to(slotted, (expert_count, ES, capacity, feature_width))]
  transfers between devices with their start and end apart: 6 -> 18, of which waited for: 5 -> 7; matrix products, arithmetic and copies ran while one was open for 15% -> 28% of each run, Pallas kernels for 0% -> 0%
where the time goes in v1:
time: 263 us; the launch traced here: 261 us
  waiting for transfers between devices  148 us (56%)
  local copies, waits for them, and re-layouts  39 us (15%)
  matrix products  33.9 us (13%)
  starting transfers between devices  28.1 us (11%)
  other arithmetic  11.6 us (4%)
    ppermute x14, waiting for transfers between devices, exchange_in_pairs(): lax.ppermute(sent, axis, [(i, i ^ turn) for i in range(devices)])  87.8 us
    all_to_all x2, waiting for transfers between devices, expert_pass(): lax.all_to_all(partial_value, 'ep', split_axis=0, concat_axis=0, tiled=True)  37.4 us
    unnamed x32, local copies, waits for them, and re-layouts  23.5 us
    ppermute x2, waiting for transfers between devices, from_behind(): return lax.ppermute(value, axis, pairs)  22.6 us
    dot_general x2, matrix products, expert_pass(): jnp.dot(hidden, down_part, preferred_element_type=jnp.float32)  18.2 us
    ppermute x14, starting transfers between devices, exchange_in_pairs(): lax.ppermute(sent, axis, [(i, i ^ turn) for i in range(devices)])  11.4 us
    all_to_all x2, starting transfers between devices, expert_pass(): lax.all_to_all(partial_value, 'ep', split_axis=0, concat_axis=0, tiled=True)  11.4 us
    gather x2, local copies, waits for them, and re-layouts, exchange_in_pairs(): tiles = jnp.stack(gathered)[here ^ jnp.arange(devices)]  9.79 us
  transfers between devices with their start and end apart: 18, of which 7 were waited for; matrix products, arithmetic and copies ran while one was open for 28% of the time, Pallas kernels for 0%

profile of v1, /device:TPU:2, one launch (start us, length us, event | category | flops | bytes accessed | tf_op | source)
XLA Modules:
  0.0 261.5 jit_solution(16318456171257961046)
XLA Ops:
  7.5 2.0 dynamic-slice_bitcast_fusion
  9.5 1.9 collective-permute-start.10
  17.6 1.9 bitcast_dynamic-update-slice_fusion.6
  19.5 4.9 %collective-permute-done.9 = bf16[1,72,3584]{2,1,0:T(8,128)(2,1)} collective-permute-done((bf16[1,72,3584]{2,1,0:T(8,128)(2,1)}, bf16[1,72,3584]{2,1,0:T(8,128)(2,1)}, u32[]{:S(2)}, u32[]{:S(2)}) %collective-permute-start.9) | collective-permute-done | bytes 516128 | tf_op jit(solution)/shard_map/ppermute | solution.py:28
  24.7 1.9 bitcast_dynamic-update-slice_fusion.5
  26.6 8.0 %collective-permute-done.10 = bf16[1,72,3584]{2,1,0:T(8,128)(2,1)} collective-permute-done((bf16[1,72,3584]{2,1,0:T(8,128)(2,1)}, bf16[1,72,3584]{2,1,0:T(8,128)(2,1)}, u32[]{:S(2)}, u32[]{:S(2)}) %collective-permute-start.10) | collective-permute-done | bytes 516128 | tf_op jit(solution)/shard_map/ppermute | solution.py:28
  35.6 1.9 bitcast_dynamic-update-slice_fusion.4
  37.5 1.9 bitcast_dynamic-update-slice_fusion.3
  39.4 18.5 %collective-permute-done.12 = bf16[1,72,3584]{2,1,0:T(8,128)(2,1)} collective-permute-done((bf16[1,72,3584]{2,1,0:T(8,128)(2,1)}, bf16[1,72,3584]{2,1,0:T(8,128)(2,1)}, u32[]{:S(2)}, u32[]{:S(2)}) %collective-permute-start.12) | collective-permute-done | bytes 516128 | tf_op jit(solution)/shard_map/ppermute | solution.py:28
  58.8 1.9 bitcast_dynamic-update-slice_fusion.2
  64.1 4.9 %gather_fusion.1 = bf16[8,72,3584]{2,1,0:T(8,128)(2,1)} fusion(bf16[8,72,3584]{2,1,0:T(8,128)(2,1)} %bitcast.54, s32[1024]{0:T(1024)S(1)} %pad_clamp_fusion), kind=kCustom, calls=%fused_computation.1 | custom fusion | bytes 8257568 | tf_op jit(solution)/shard_map/gather | solution.py:29
  69.0 4.8 %fusion.12 = f32[576,256]{1,0:T(8,128)} fusion(bf16[576,3584]{1,0:T(8,128)(2,1)} %bitcast.152, bf16[1,3584,256]{2,1,0:T(8,128)(2,1)} %param.17), kind=kOutput, calls=%fused_computation.24 | convolution fusion | flops 1056964608 | bytes 6553600 | tf_op jit(solution)/shard_map/dot_general | solution.py:77
  73.8 9.2 %convolution_convert_fusion = bf16[576,3584]{1,0:T(8,128)(2,1)} fusion(bf16[1,256,3584]{2,1,0:T(8,128)(2,1)S(1)} %copy-done, bf16[576,3584]{1,0:T(8,128)(2,1)} %bitcast.153, bf16[1,3584,256]{2,1,0:T(8,128)(2,1)} %param.18, f32[576,256]{1,0:T(8,128)} %fusion.12), kind=kOutput, calls=%fused_computation.4 | convolution fusion | flops 2116878336 | bytes 12517376 | tf_op jit(solution)/shard_map/dot_general | solution.py:80
  83.0 5.9 %all-to-all-start.1 = ((bf16[8,72,3584]{2,1,0:T(8,128)(2,1)}), bf16[8,72,3584]{2,1,0:T(8,128)(2,1)}, u32[]{:S(2)}, u32[]{:S(2)}) async-start(bf16[8,72,3584]{2,1,0:T(8,128)(2,1)} %bitcast.148), calls=%async_computation.1 | async-start | bytes 8257536 | tf_op jit(solution)/shard_map/all_to_all | solution.py:84
  93.2 1.9 bitcast_dynamic-update-slice_fusion.12
  95.0 1.9 bitcast_dynamic-update-slice_fusion.11
  96.9 1.9 bitcast_dynamic-update-slice_fusion.10
  98.8 1.9 bitcast_dynamic-update-slice_fusion.9
  100.6 46.9 %collective-permute-done.5 = bf16[1,72,3584]{2,1,0:T(8,128)(2,1)S(1)} collective-permute-done((bf16[1,72,3584]{2,1,0:T(8,128)(2,1)S(1)}, bf16[1,72,3584]{2,1,0:T(8,128)(2,1)S(1)}, u32[]{:S(2)}, u32[]{:S(2)}) %collective-permute-start.5) | collective-permute-done | bytes 516128 | tf_op jit(solution)/shard_map/ppermute | solution.py:28
  148.4 9.5 %collective-permute-done.6 = bf16[1,72,3584]{2,1,0:T(8,128)(2,1)S(1)} collective-permute-done((bf16[1,72,3584]{2,1,0:T(8,128)(2,1)S(1)}, bf16[1,72,3584]{2,1,0:T(8,128)(2,1)S(1)}, u32[]{:S(2)}, u32[]{:S(2)}) %collective-permute-start.6) | collective-permute-done | bytes 516128 | tf_op jit(solution)/shard_map/ppermute | solution.py:28
  158.7 4.9 %gather_fusion = bf16[8,72,3584]{2,1,0:T(8,128)(2,1)} fusion(bf16[8,72,3584]{2,1,0:T(8,128)(2,1)} %bitcast.145, s32[1024]{0:T(1024)S(1)} %pad_clamp_fusion), kind=kCustom, calls=%fused_computation | custom fusion | bytes 8257568 | tf_op jit(solution)/shard_map/gather | solution.py:29
  163.6 4.0 %fusion.14 = f32[576,256]{1,0:T(8,128)S(1)} fusion(bf16[576,3584]{1,0:T(8,128)(2,1)} %bitcast.150, bf16[1,3584,256]{2,1,0:T(8,128)(2,1)} %param.17), kind=kOutput, calls=%fused_computation.26 | convolution fusion | flops 1056964608 | bytes 6553600 | tf_op jit(solution)/shard_map/dot_general | solution.py:77
  167.6 9.1 %convolution_convert_fusion.1 = bf16[576,3584]{1,0:T(8,128)(2,1)} fusion(bf16[1,256,3584]{2,1,0:T(8,128)(2,1)S(1)} %copy-done, bf16[576,3584]{1,0:T(8,128)(2,1)} %bitcast.151, bf16[1,3584,256]{2,1,0:T(8,128)(2,1)} %param.18, f32[576,256]{1,0:T(8,128)S(1)} %fusion.14), kind=kOutput, calls=%fused_computation.5 | convolution fusion | flops 2116878336 | bytes 12517376 | tf_op jit(solution)/shard_map/dot_general | solution.py:80
  176.6 5.5 %all-to-all-start = ((bf16[8,72,3584]{2,1,0:T(8,128)(2,1)}), bf16[8,72,3584]{2,1,0:T(8,128)(2,1)}, u32[]{:S(2)}, u32[]{:S(2)}) async-start(bf16[8,72,3584]{2,1,0:T(8,128)(2,1)} %bitcast.149), calls=%async_computation | async-start | bytes 8257536 | tf_op jit(solution)/shard_map/all_to_all | solution.py:84
  182.2 3.1 %convert_reduce_fusion = f32[2,72,3584]{2,1,0:T(8,128)S(1)} fusion(bf16[8,72,3584]{2,1,0:T(8,128)(2,1)} %all-to-all-done.1), kind=kLoop, calls=%fused_computation.2 | loop fusion | flops 3612672 | bytes 6193152 | tf_op jit(solution)/shard_map/reduce_sum | solution.py:91
  185.3 2.8 %fusion.2 = bf16[128,3584]{1,0:T(8,128)(2,1)} fusion(f32[144,3584]{1,0:T(8,128)S(1)} %bitcast.143, bf16[1,128,3584]{2,1,0:T(8,128)(2,1)S(1)} %copy-done.1, pred[]{:T(512)S(6)} %le.3, f32[128]{0:T(128)S(1)} %bitcast.159, s32[128]{0:T(128)S(1)} %multiply_add_fusion), kind=kOutput, calls=%fused_computation.12 | convolution fusion | flops 794595328 | bytes 3900417 | tf_op jit(solution)/shard_map/dot_general | solution.py:92
  188.1 3.6 %collective-permute-start.15 = (bf16[128,3584]{1,0:T(8,128)(2,1)}, bf16[128,3584]{1,0:T(8,128)(2,1)}, u32[]{:S(2)}, u32[]{:S(2)}) collective-permute-start(bf16[128,3584]{1,0:T(8,128)(2,1)} %fusion.2), channel_id=1, source_target_pairs={{0,24},{8,0},{16,8},{24,16},{1,25},{9,1},{17,9},{25,17},{2,26},{10... | collective-permute-start | bytes 2752520 | tf_op jit(solution)/shard_map/ppermute | solution.py:36
  191.7 37.4 %all-to-all-done = bf16[8,72,3584]{2,1,0:T(8,128)(2,1)} async-done(((bf16[8,72,3584]{2,1,0:T(8,128)(2,1)}), bf16[8,72,3584]{2,1,0:T(8,128)(2,1)}, u32[]{:S(2)}, u32[]{:S(2)}) %all-to-all-start) | async-done | bytes 4128800 | tf_op jit(solution)/shard_map/all_to_all | solution.py:84
  229.2 3.1 %convert_reduce_fusion.1 = f32[2,72,3584]{2,1,0:T(8,128)S(1)} fusion(bf16[8,72,3584]{2,1,0:T(8,128)(2,1)} %all-to-all-done), kind=kLoop, calls=%fused_computation.3 | loop fusion | flops 3612672 | bytes 6193152 | tf_op jit(solution)/shard_map/reduce_sum | solution.py:91
  232.2 1.9 fusion.3
  235.8 22.6 %collective-permute-done.7 = bf16[128,3584]{1,0:T(8,128)(2,1)S(1)} collective-permute-done((bf16[128,3584]{1,0:T(8,128)(2,1)S(1)}, bf16[128,3584]{1,0:T(8,128)(2,1)S(1)}, u32[]{:S(2)}, u32[]{:S(2)}) %collective-permute-start.7) | collective-permute-done | bytes 917536 | tf_op jit(solution)/shard_map/ppermute | solution.py:36
  259.3 2.2 copy.29
  (69 shorter events, 27.1 us)
Async XLA Ops:
  0.6 73.2 %copy-start = (bf16[1,256,3584]{2,1,0:T(8,128)(2,1)S(1)}, bf16[1,256,3584]{2,1,0:T(8,128)(2,1)}, u32[]{:S(2)}) copy-start(bf16[1,256,3584]{2,1,0:T(8,128)(2,1)} %param.19) | copy-start | bytes 5505028
  7.5 5.6 %copy-start.6 = (s32[1,1,128,1]{2,3,1,0:T(1,128)S(1)}, s32[1,1,128,1]{2,3,1,0:T(1,128)}, u32[]{:S(2)}) copy-start(s32[1,1,128,1]{2,3,1,0:T(1,128)} %param.12) | copy-start | bytes 1540
  7.5 6.0 %copy-start.2 = (bf16[1,128,3584]{2,1,0:T(8,128)(2,1)S(1)}, bf16[1,128,3584]{2,1,0:T(8,128)(2,1)}, u32[]{:S(2)}) copy-start(bf16[1,128,3584]{2,1,0:T(8,128)(2,1)} %param.10) | copy-start | bytes 2752516
  9.5 6.6 %collective-permute-start.8 = (bf16[1,72,3584]{2,1,0:T(8,128)(2,1)}, bf16[1,72,3584]{2,1,0:T(8,128)(2,1)}, u32[]{:S(2)}, u32[]{:S(2)}) collective-permute-start(bf16[1,72,3584]{2,1,0:T(8,128)(2,1)} %get-tuple-element.8), channel_id=1, source_target_pairs={{0,1},{1,0},{2,3},{3,2},{4,5},{5,4},{6,7},{7,6},{8,9},{9,8},{10,11... | collective-permute-start | bytes 1548296 | tf_op jit(solution)/shard_map/ppermute | solution.py:28
  9.5 14.9 %collective-permute-start.9 = (bf16[1,72,3584]{2,1,0:T(8,128)(2,1)}, bf16[1,72,3584]{2,1,0:T(8,128)(2,1)}, u32[]{:S(2)}, u32[]{:S(2)}) collective-permute-start(bf16[1,72,3584]{2,1,0:T(8,128)(2,1)} %get-tuple-element.7), channel_id=1, source_target_pairs={{0,2},{1,3},{2,0},{3,1},{4,6},{5,7},{6,4},{7,5},{8,10},{9,11},{10,... | collective-permute-start | bytes 1548296 | tf_op jit(solution)/shard_map/ppermute | solution.py:28
  9.5 25.1 %collective-permute-start.10 = (bf16[1,72,3584]{2,1,0:T(8,128)(2,1)}, bf16[1,72,3584]{2,1,0:T(8,128)(2,1)}, u32[]{:S(2)}, u32[]{:S(2)}) collective-permute-start(bf16[1,72,3584]{2,1,0:T(8,128)(2,1)} %get-tuple-element.6), channel_id=1, source_target_pairs={{0,3},{1,2},{2,1},{3,0},{4,7},{5,6},{6,5},{7,4},{8,11},{9,10},{10,... | collective-permute-start | bytes 1548296 | tf_op jit(solution)/shard_map/ppermute | solution.py:28
  11.4 26.1 %collective-permute-start.11 = (bf16[1,72,3584]{2,1,0:T(8,128)(2,1)}, bf16[1,72,3584]{2,1,0:T(8,128)(2,1)}, u32[]{:S(2)}, u32[]{:S(2)}) collective-permute-start(bf16[1,72,3584]{2,1,0:T(8,128)(2,1)} %get-tuple-element.5), channel_id=1, source_target_pairs={{0,4},{1,5},{2,6},{3,7},{4,0},{5,1},{6,2},{7,3},{8,12},{9,13},{10,... | collective-permute-start | bytes 1548296 | tf_op jit(solution)/shard_map/ppermute | solution.py:28
  12.9 45.0 %collective-permute-start.12 = (bf16[1,72,3584]{2,1,0:T(8,128)(2,1)}, bf16[1,72,3584]{2,1,0:T(8,128)(2,1)}, u32[]{:S(2)}, u32[]{:S(2)}) collective-permute-start(bf16[1,72,3584]{2,1,0:T(8,128)(2,1)} %get-tuple-element.4), channel_id=1, source_target_pairs={{0,5},{1,4},{2,7},{3,6},{4,1},{5,0},{6,3},{7,2},{8,13},{9,12},{10,... | collective-permute-start | bytes 1548296 | tf_op jit(solution)/shard_map/ppermute | solution.py:28
  14.6 1.5 copy-start.5
  14.6 9.9 %copy-start.4 = (bf16[1,72,3584]{2,1,0:T(8,128)(2,1)S(1)}, bf16[1,72,3584]{2,1,0:T(8,128)(2,1)}, u32[]{:S(2)}) copy-start(bf16[1,72,3584]{2,1,0:T(8,128)(2,1)} %get-tuple-element.2) | copy-start | bytes 1548292
  16.1 44.5 %collective-permute-start.13 = (bf16[1,72,3584]{2,1,0:T(8,128)(2,1)S(1)}, bf16[1,72,3584]{2,1,0:T(8,128)(2,1)S(1)}, u32[]{:S(2)}, u32[]{:S(2)}) collective-permute-start(bf16[1,72,3584]{2,1,0:T(8,128)(2,1)S(1)} %copy-done.5), channel_id=1, source_target_pairs={{0,6},{1,7},{2,4},{3,5},{4,2},{5,3},{6,0},{7,1},{8,14},{9,15},{10,... | collective-permute-start | bytes 1548296 | tf_op jit(solution)/shard_map/ppermute | solution.py:28
  24.5 38.8 %collective-permute-start.14 = (bf16[1,72,3584]{2,1,0:T(8,128)(2,1)S(1)}, bf16[1,72,3584]{2,1,0:T(8,128)(2,1)S(1)}, u32[]{:S(2)}, u32[]{:S(2)}) collective-permute-start(bf16[1,72,3584]{2,1,0:T(8,128)(2,1)S(1)} %copy-done.4), channel_id=1, source_target_pairs={{0,7},{1,6},{2,5},{3,4},{4,3},{5,2},{6,1},{7,0},{8,15},{9,14},{10,... | collective-permute-start | bytes 1548296 | tf_op jit(solution)/shard_map/ppermute | solution.py:28
  34.6 54.3 %collective-permute-start = (bf16[1,72,3584]{2,1,0:T(8,128)(2,1)}, bf16[1,72,3584]{2,1,0:T(8,128)(2,1)}, u32[]{:S(2)}, u32[]{:S(2)}) collective-permute-start(bf16[1,72,3584]{2,1,0:T(8,128)(2,1)} %get-tuple-element.16), channel_id=1, source_target_pairs={{0,1},{1,0},{2,3},{3,2},{4,5},{5,4},{6,7},{7,6},{8,9},{9,8},{10,11... | collective-permute-start | bytes 1548296 | tf_op jit(solution)/shard_map/ppermute | solution.py:28
  37.5 54.8 %collective-permute-start.1 = (bf16[1,72,3584]{2,1,0:T(8,128)(2,1)}, bf16[1,72,3584]{2,1,0:T(8,128)(2,1)}, u32[]{:S(2)}, u32[]{:S(2)}) collective-permute-start(bf16[1,72,3584]{2,1,0:T(8,128)(2,1)} %get-tuple-element.15), channel_id=1, source_target_pairs={{0,2},{1,3},{2,0},{3,1},{4,6},{5,7},{6,4},{7,5},{8,10},{9,11},{10,... | collective-permute-start | bytes 1548296 | tf_op jit(solution)/shard_map/ppermute | solution.py:28
  57.8 37.2 %collective-permute-start.2 = (bf16[1,72,3584]{2,1,0:T(8,128)(2,1)}, bf16[1,72,3584]{2,1,0:T(8,128)(2,1)}, u32[]{:S(2)}, u32[]{:S(2)}) collective-permute-start(bf16[1,72,3584]{2,1,0:T(8,128)(2,1)} %get-tuple-element.14), channel_id=1, source_target_pairs={{0,3},{1,2},{2,1},{3,0},{4,7},{5,6},{6,5},{7,4},{8,11},{9,10},{10,... | collective-permute-start | bytes 1548296 | tf_op jit(solution)/shard_map/ppermute | solution.py:28
  60.7 36.2 %collective-permute-start.3 = (bf16[1,72,3584]{2,1,0:T(8,128)(2,1)}, bf16[1,72,3584]{2,1,0:T(8,128)(2,1)}, u32[]{:S(2)}, u32[]{:S(2)}) collective-permute-start(bf16[1,72,3584]{2,1,0:T(8,128)(2,1)} %get-tuple-element.13), channel_id=1, source_target_pairs={{0,4},{1,5},{2,6},{3,7},{4,0},{5,1},{6,2},{7,3},{8,12},{9,13},{10,... | collective-permute-start | bytes 1548296 | tf_op jit(solution)/shard_map/ppermute | solution.py:28
  63.3 35.5 %collective-permute-start.4 = (bf16[1,72,3584]{2,1,0:T(8,128)(2,1)S(1)}, bf16[1,72,3584]{2,1,0:T(8,128)(2,1)}, u32[]{:S(2)}, u32[]{:S(2)}) collective-permute-start(bf16[1,72,3584]{2,1,0:T(8,128)(2,1)S(1)} %get-tuple-element.12), channel_id=1, source_target_pairs={{0,5},{1,4},{2,7},{3,6},{4,1},{5,0},{6,3},{7,2},{8,13},{9,12},{10,... | collective-permute-start | bytes 1548296 | tf_op jit(solution)/shard_map/ppermute | solution.py:28
  83.0 93.6 %all-to-all-start.1 = ((bf16[8,72,3584]{2,1,0:T(8,128)(2,1)}), bf16[8,72,3584]{2,1,0:T(8,128)(2,1)}, u32[]{:S(2)}, u32[]{:S(2)}) async-start(bf16[8,72,3584]{2,1,0:T(8,128)(2,1)} %bitcast.148), calls=%async_computation.1 | async-start | bytes 8257536 | tf_op jit(solution)/shard_map/all_to_all | solution.py:84
  88.9 58.6 %collective-permute-start.5 = (bf16[1,72,3584]{2,1,0:T(8,128)(2,1)S(1)}, bf16[1,72,3584]{2,1,0:T(8,128)(2,1)S(1)}, u32[]{:S(2)}, u32[]{:S(2)}) collective-permute-start(bf16[1,72,3584]{2,1,0:T(8,128)(2,1)S(1)} %get-tuple-element.11), channel_id=1, source_target_pairs={{0,6},{1,7},{2,4},{3,5},{4,2},{5,3},{6,0},{7,1},{8,14},{9,15},{10,... | collective-permute-start | bytes 1548296 | tf_op jit(solution)/shard_map/ppermute | solution.py:28
  92.3 65.6 %collective-permute-start.6 = (bf16[1,72,3584]{2,1,0:T(8,128)(2,1)S(1)}, bf16[1,72,3584]{2,1,0:T(8,128)(2,1)S(1)}, u32[]{:S(2)}, u32[]{:S(2)}) collective-permute-start(bf16[1,72,3584]{2,1,0:T(8,128)(2,1)S(1)} %get-tuple-element.10), channel_id=1, source_target_pairs={{0,7},{1,6},{2,5},{3,4},{4,3},{5,2},{6,1},{7,0},{8,15},{9,14},{10,... | collective-permute-start | bytes 1548296 | tf_op jit(solution)/shard_map/ppermute | solution.py:28
  176.6 52.5 %all-to-all-start = ((bf16[8,72,3584]{2,1,0:T(8,128)(2,1)}), bf16[8,72,3584]{2,1,0:T(8,128)(2,1)}, u32[]{:S(2)}, u32[]{:S(2)}) async-start(bf16[8,72,3584]{2,1,0:T(8,128)(2,1)} %bitcast.149), calls=%async_computation | async-start | bytes 8257536 | tf_op jit(solution)/shard_map/all_to_all | solution.py:84
  182.2 3.1 %copy-start.1 = (bf16[1,128,3584]{2,1,0:T(8,128)(2,1)S(1)}, bf16[1,128,3584]{2,1,0:T(8,128)(2,1)}, u32[]{:S(2)}) copy-start(bf16[1,128,3584]{2,1,0:T(8,128)(2,1)} %param.11) | copy-start | bytes 2752516
  182.2 3.1 %copy-start.7 = (f32[1,1,128,1]{2,3,1,0:T(1,128)S(1)}, f32[1,1,128,1]{2,3,1,0:T(1,128)}, u32[]{:S(2)}) copy-start(f32[1,1,128,1]{2,3,1,0:T(1,128)} %param.15) | copy-start | bytes 1540
  185.3 46.9 %copy-start.8 = (f32[1,1,128,1]{2,3,1,0:T(1,128)S(1)}, f32[1,1,128,1]{2,3,1,0:T(1,128)}, u32[]{:S(2)}) copy-start(f32[1,1,128,1]{2,3,1,0:T(1,128)} %param.14) | copy-start | bytes 1540
  188.1 44.1 %copy-start.3 = (bf16[1,128,3584]{2,1,0:T(8,128)(2,1)S(1)}, bf16[1,128,3584]{2,1,0:T(8,128)(2,1)}, u32[]{:S(2)}) copy-start(bf16[1,128,3584]{2,1,0:T(8,128)(2,1)} %param.10) | copy-start | bytes 2752516
  188.1 47.7 %collective-permute-start.15 = (bf16[128,3584]{1,0:T(8,128)(2,1)}, bf16[128,3584]{1,0:T(8,128)(2,1)}, u32[]{:S(2)}, u32[]{:S(2)}) collective-permute-start(bf16[128,3584]{1,0:T(8,128)(2,1)} %fusion.2), channel_id=1, source_target_pairs={{0,24},{8,0},{16,8},{24,16},{1,25},{9,1},{17,9},{25,17},{2,26},{10... | collective-permute-start | bytes 2752520 | tf_op jit(solution)/shard_map/ppermute | solution.py:36
  234.2 24.2 %collective-permute-start.7 = (bf16[128,3584]{1,0:T(8,128)(2,1)S(1)}, bf16[128,3584]{1,0:T(8,128)(2,1)S(1)}, u32[]{:S(2)}, u32[]{:S(2)}) collective-permute-start(bf16[128,3584]{1,0:T(8,128)(2,1)S(1)} %fusion.3), channel_id=1, source_target_pairs={{0,8},{8,16},{16,24},{24,0},{1,9},{9,17},{17,25},{25,1},{2,10},{10... | collective-permute-start | bytes 2752520 | tf_op jit(solution)/shard_map/ppermute | solution.py:36
